TPU v7x, 512 devices: a whole 4x8x8 slice. The times are simulated.
512 devices in a mesh: de: 32 (over x, y_lo, core), et: 16 (over y_hi, z).
Axes of the slice: x: 4, y: 8 (y_hi: 2, y_lo: 4; y = y_hi * 4 + y_lo), z: 8, core: 2. Of those that a mesh axis runs over, the one named last changes fastest.
Arguments:
- tokens: bfloat16 [256, 6144], P('de', 'et'), may hold values from -6 to 6
- expert_ids: int32 [256, 2], P('de'), may hold values from 0 to 3, all different within a row; in each aligned block of 8 rows (0 to 7, 8 to 15, ...) at most 5 rows name the same one
- gate_probs: float32 [256, 2], P('de'), may hold values from 0.1 to 1
- w_gate: bfloat16 [6144, 65536], P(None, ('de', 'et')), may hold values from -0.078125 to 0.078125
- w_up: bfloat16 [6144, 65536], P(None, ('de', 'et')), may hold values from -0.078125 to 0.078125
- w_down: bfloat16 [65536, 6144], P(('de', 'et')), may hold values from -0.046875 to 0.046875
- out_grad: bfloat16 [256, 6144], P('de', 'et'), may hold values from -6 to 6
Outputs:
- mixed: bfloat16 [256, 6144], P('de', 'et')
- token_grad: bfloat16 [256, 6144], P('de', 'et')
- prob_grad: float32 [256, 2], P('de')
Inputs may be any that keep to these rules, and one draw needn't show every extreme that they name: `expert_ids`: the 2 entries of a token are different. Among the 8 tokens of one index of de, no expert is named by more than 5 tokens, a bound that some expert reaches in some of these blocks.
All inputs are finite; a program needn't handle non-finite values.
Results may differ from a plain program's by a relative error of at most 0.02.
Values may be sent and summed in bfloat16 or wider, within the bound.
A program may use at most 64 MiB of HBM per device.

v0:
```python
import jax
import jax.numpy as jnp
from jax import lax
from jax.sharding import PartitionSpec as P

EXPERTS = 4
CAP = 5


def activate(gate, up, d_hidden):
    sig = jax.nn.sigmoid(gate)
    hidden = (gate * sig * up).astype(jnp.bfloat16)
    d_gate = (d_hidden * up * sig * (1.0 + gate * (1.0 - sig))).astype(jnp.bfloat16)
    d_up = (d_hidden * gate * sig).astype(jnp.bfloat16)
    return (hidden, d_gate, d_up)


def input_terms(d_gate, d_up, w_gate, w_up):
    first = lax.dot_general(
        d_gate, w_gate, (((1,), (1,)), ((), ())), preferred_element_type=jnp.float32
    )
    return first + lax.dot_general(
        d_up, w_up, (((1,), (1,)), ((), ())), preferred_element_type=jnp.float32
    )


def body(tokens, expert_ids, gate_probs, w_gate, w_up, w_down, out_grad):
    n_de = lax.axis_size("de")
    members = n_de // EXPERTS
    width = tokens.shape[1]
    picks = (expert_ids[:, :, None] == jnp.arange(EXPERTS, dtype=jnp.int32)[None, None, :]).astype(
        jnp.float32
    )
    named = jnp.sum(picks, axis=1)
    weight = jnp.sum(picks * gate_probs[:, :, None], axis=1)
    rank = jnp.cumsum(named.astype(jnp.int32), axis=0) - 1
    place = named.T[:, None, :] * (
        rank.T[:, None, :] == jnp.arange(CAP, dtype=jnp.int32)[None, :, None]
    ).astype(jnp.float32)
    grad_f = out_grad.astype(jnp.float32)
    highest = lax.Precision.HIGHEST
    x_slots = jnp.einsum(
        "ect,td->ecd", place, tokens.astype(jnp.float32), precision=highest
    ).astype(jnp.bfloat16)
    scaled = weight[:, :, None] * grad_f[:, None, :]
    g_slots = jnp.einsum("ect,ted->ecd", place, scaled, precision=highest).astype(jnp.bfloat16)
    x_send = jnp.repeat(x_slots, members, axis=0).reshape(n_de * CAP, width)
    g_send = jnp.repeat(g_slots, members, axis=0).reshape(n_de * CAP, width)
    x_recv, g_recv = (
        lax.all_to_all(x_send, "de", split_axis=0, concat_axis=0, tiled=True),
        lax.all_to_all(g_send, "de", split_axis=0, concat_axis=0, tiled=True),
    )
    x_piece = lax.all_gather(x_recv, "et", axis=1, tiled=True)
    g_piece = lax.all_gather(g_recv, "et", axis=1, tiled=True)
    gate = jnp.dot(x_piece, w_gate, preferred_element_type=jnp.float32)
    up = jnp.dot(x_piece, w_up, preferred_element_type=jnp.float32)
    back = lax.dot_general(
        g_piece, w_down, (((1,), (1,)), ((), ())), preferred_element_type=jnp.float32
    )
    gate, up, d_hidden = (gate, up, back)
    hidden, d_gate, d_up = activate(gate, up, d_hidden)
    y_term = jnp.dot(hidden, w_down, preferred_element_type=jnp.float32)
    x_term = input_terms(d_gate, d_up, w_gate, w_up)
    y_part, x_part = (
        lax.psum_scatter(y_term.astype(jnp.bfloat16), "et", scatter_dimension=1, tiled=True).astype(
            jnp.float32
        ),
        lax.psum_scatter(x_term.astype(jnp.bfloat16), "et", scatter_dimension=1, tiled=True).astype(
            jnp.float32
        ),
    )
    y_back, x_back = (
        lax.all_to_all(
            y_part.astype(jnp.bfloat16), "de", split_axis=0, concat_axis=0, tiled=True
        ).astype(y_part.dtype),
        lax.all_to_all(
            x_part.astype(jnp.bfloat16), "de", split_axis=0, concat_axis=0, tiled=True
        ).astype(x_part.dtype),
    )
    y_sum = jnp.sum(y_back.reshape(EXPERTS, members, CAP, width), axis=1)
    x_sum = jnp.sum(x_back.reshape(EXPERTS, members, CAP, width), axis=1)
    weighted = place * weight.T[:, None, :]
    mixed = jnp.einsum("ect,ecd->td", weighted, y_sum, precision=highest).astype(jnp.bfloat16)
    token_grad = jnp.einsum("ect,ecd->td", place, x_sum, precision=highest).astype(jnp.bfloat16)
    products = jnp.einsum("ecd,td->ect", y_sum, grad_f, precision=highest)
    scores = jnp.sum(place * products, axis=1).T
    partial_grad = jnp.sum(picks * scores[:, None, :], axis=2)
    prob_grad = lax.psum(partial_grad, "et")
    return (mixed, token_grad, prob_grad)


def solution(mesh):
    return jax.shard_map(
        body,
        mesh=mesh,
        in_specs=(
            P("de", "et"),
            P("de", None),
            P("de", None),
            P(None, ("de", "et")),
            P(None, ("de", "et")),
            P(("de", "et"), None),
            P("de", "et"),
        ),
        out_specs=(P("de", "et"), P("de", "et"), P("de", None)),
        check_vma=False,
    )
```

profile of v0, /device:TPU:1, one launch (start us, length us, event | category | flops | bytes accessed | tf_op | source)
XLA Modules:
  0.0 785.1 jit_solution(16925550155666623164)
XLA Ops:
  7.2 0.0 copy-start
  7.2 0.0 all-gather.3.cloned.1.call-start
  7.2 0.8 convert_reduce_fusion.2
  8.0 0.2 reduce_window_sum.11
  8.2 0.8 convolution_convert_fusion.2
  9.1 19.5 %all_to_all.42 = bf16[32,5,384]{2,1,0:T(8,128)(2,1)S(1)} all-to-all(bf16[32,5,384]{2,1,0:T(8,128)(2,1)S(1)} %bitcast.45), channel_id=1, replica_groups=mesh['de'=32,'et'=16] {'de'}, dimensions={0} | all-to-all | bytes 245760 | tf_op jit(solution)/shard_map/all_to_all | solution.py:50
  28.6 0.0 copy-start.3
  28.6 0.7 all_to_all.30
  29.3 0.0 all-gather.3.cloned.1.call-update
  29.3 0.0 reduce-scatter.7.cloned.1.call-start
  29.4 95.4 %all-gather.3.cloned.1.call-done = bf16[160,6144]{1,0:T(8,128)(2,1)} async-done(((bf16[160,384]{1,0:T(8,128)(2,1)}), bf16[160,6144]{1,0:T(8,128)(2,1)}) %all-gather.3.cloned.1.call-update) | async-done | bytes 1966096 | tf_op jit(solution)/shard_map/all_gather | solution.py:53
  124.8 0.0 copy-start.1
  124.8 2.8 fusion.36
  127.6 0.0 copy-done.3
  127.6 0.0 copy-done.1
  127.6 0.0 copy-start.5
  127.6 0.7 fusion.37
  128.3 0.0 copy-done.5
  128.3 0.0 copy-start.8
  128.3 0.6 copy-done.8
  128.9 0.0 copy-done
  128.9 0.7 convolution_convert_fusion
  129.6 2.7 copy.27
  132.3 0.0 copy-start.12
  132.3 0.0 reduce-scatter.7.cloned.1.call-update
  132.4 226.9 %reduce-scatter.7.cloned.1.call-done = bf16[384,160]{1,0:T(8,128)(2,1)} async-done(((bf16[6144,160]{1,0:T(8,128)(2,1)}), bf16[384,160]{1,0:T(8,128)(2,1)}) %reduce-scatter.7.cloned.1.call-update) | async-done | bytes 122896
  359.2 1.1 copy.28
  360.3 0.7 all_to_all.31
  361.0 10.9 %all-to-all-start.1 = ((bf16[32,5,384]{2,1,0:T(8,128)(2,1)}), bf16[32,5,384]{2,1,0:T(8,128)(2,1)S(1)}, u32[]{:S(2)}, u32[]{:S(2)}) async-start(bf16[32,5,384]{2,1,0:T(8,128)(2,1)} %all_to_all.31), calls=%async_computation.1 | async-start | bytes 393216 | tf_op jit(solution)/shard_map/all_to_all | solution.py:73
  371.9 0.0 all-gather.5.cloned.1.call-start
  372.0 0.0 copy-done.12
  372.0 9.8 %all-to-all-done.1 = bf16[32,5,384]{2,1,0:T(8,128)(2,1)S(1)} async-done(((bf16[32,5,384]{2,1,0:T(8,128)(2,1)}), bf16[32,5,384]{2,1,0:T(8,128)(2,1)S(1)}, u32[]{:S(2)}, u32[]{:S(2)}) %all-to-all-start.1) | async-done | bytes 122912 | tf_op jit(solution)/shard_map/all_to_all | solution.py:73
  381.9 0.0 copy-start.10
  381.9 0.2 fusion.3
  382.1 0.0 copy-done.13
  382.1 0.0 copy-done.14
  382.1 0.4 copy-done.10
  382.5 0.3 convolution_convert_fusion.1
  382.8 13.3 %all_to_all.43 = bf16[32,5,384]{2,1,0:T(8,128)(2,1)S(1)} all-to-all(bf16[32,5,384]{2,1,0:T(8,128)(2,1)S(1)} %bitcast.46), channel_id=1, replica_groups=mesh['de'=32,'et'=16] {'de'}, dimensions={0} | all-to-all | bytes 245760 | tf_op jit(solution)/shard_map/all_to_all | solution.py:51
  396.1 0.7 all_to_all.35
  396.8 0.0 all-gather.5.cloned.1.call-update
  396.8 0.0 reduce-scatter.9.cloned.1.call-start
  396.9 90.2 %all-gather.5.cloned.1.call-done = bf16[160,6144]{1,0:T(8,128)(2,1)} async-done(((bf16[160,384]{1,0:T(8,128)(2,1)}), bf16[160,6144]{1,0:T(8,128)(2,1)}) %all-gather.5.cloned.1.call-update) | async-done | bytes 1966096 | tf_op jit(solution)/shard_map/all_gather | solution.py:54
  487.0 2.2 fusion.38
  489.2 0.0 copy-done.2
  489.3 0.0 copy-done.6
  489.3 0.0 copy-done.9
  489.3 0.0 copy-start.4
  489.3 0.0 copy-start.7
  489.3 0.7 fusion.5
  490.0 0.7 copy-done.4
  490.7 0.0 copy-done.7
  490.7 0.7 fusion
  491.4 2.7 copy.29
  494.1 0.0 reduce-scatter.9.cloned.1.call-update
  494.1 226.7 %reduce-scatter.9.cloned.1.call-done = bf16[384,160]{1,0:T(8,128)(2,1)} async-done(((bf16[6144,160]{1,0:T(8,128)(2,1)}), bf16[384,160]{1,0:T(8,128)(2,1)}) %reduce-scatter.9.cloned.1.call-update) | async-done | bytes 122896
  720.8 1.1 copy.30
  721.9 0.7 all_to_all.36
  722.6 10.9 %all-to-all-start.3 = ((bf16[32,5,384]{2,1,0:T(8,128)(2,1)}), bf16[32,5,384]{2,1,0:T(8,128)(2,1)S(1)}, u32[]{:S(2)}, u32[]{:S(2)}) async-start(bf16[32,5,384]{2,1,0:T(8,128)(2,1)} %all_to_all.36), calls=%async_computation.3 | async-start | bytes 393216 | tf_op jit(solution)/shard_map/all_to_all | solution.py:76
  733.5 43.3 %psum.7 = f32[8,2]{0,1:T(2,128)} all-reduce(f32[8,2]{0,1:T(2,128)S(1)} %get-tuple-element.3), channel_id=1, replica_groups=mesh['de'=32,'et'=16] {'et'}, use_global_device_ids=true, to_apply=%region_9.10 | all-reduce | flops 16 | bytes 128 | tf_op jit(solution)/shard_map/psum | solution.py:88
  776.9 0.0 copy-done.11
  776.9 0.8 fusion.1
  777.7 0.0 all-to-all-done.3
  777.7 0.8 fusion.2
  (14 shorter events, 0.2 us)
Async XLA Ops:
  7.2 121.7 %copy-start = (bf16[128,6144]{1,0:T(8,128)(2,1)S(1)}, bf16[128,6144]{1,0:T(8,128)(2,1)}, u32[]{:S(2)}) copy-start(bf16[128,6144]{1,0:T(8,128)(2,1)} %param.12) | copy-start | bytes 4718596
  7.2 117.6 %all-gather.3.cloned.1.call-start = ((), (), s32[]{:S(2)}) async-start(), calls=%async_computation.6 | async-start | bytes 2088960 | tf_op jit(solution)/shard_map/all_gather | solution.py:53
  28.6 98.9 %copy-start.3 = (bf16[6144,128]{1,0:T(8,128)(2,1)S(1)}, bf16[6144,128]{1,0:T(8,128)(2,1)}, u32[]{:S(2)}) copy-start(bf16[6144,128]{1,0:T(8,128)(2,1)} %param.11) | copy-start | bytes 4718596
  29.3 329.9 %reduce-scatter.7.cloned.1.call-start = ((), (), s32[]{:S(2)}) async-start(), calls=%async_computation.8 | async-start | bytes 3342336
  124.8 2.8 copy-start.1
  127.6 0.7 copy-start.5
  128.3 0.6 copy-start.8
  132.3 239.7 %copy-start.12 = (bf16[8,384]{1,0:T(8,128)(2,1)S(1)}, bf16[8,384]{1,0:T(8,128)(2,1)}, u32[]{:S(2)}) copy-start(bf16[8,384]{1,0:T(8,128)(2,1)} %param.13) | copy-start | bytes 18436
  132.3 249.8 %copy-start.13 = (s32[8,2]{0,1:T(2,128)S(1)}, s32[8,2]{0,1:T(2,128)}, u32[]{:S(2)}) copy-start(s32[8,2]{0,1:T(2,128)} %param.8) | copy-start | bytes 196
  132.3 249.8 %copy-start.14 = (f32[8,2]{0,1:T(2,128)S(1)}, f32[8,2]{0,1:T(2,128)}, u32[]{:S(2)}) copy-start(f32[8,2]{0,1:T(2,128)} %param.9) | copy-start | bytes 196
  361.0 20.8 %all-to-all-start.1 = ((bf16[32,5,384]{2,1,0:T(8,128)(2,1)}), bf16[32,5,384]{2,1,0:T(8,128)(2,1)S(1)}, u32[]{:S(2)}, u32[]{:S(2)}) async-start(bf16[32,5,384]{2,1,0:T(8,128)(2,1)} %all_to_all.31), calls=%async_computation.1 | async-start | bytes 393216 | tf_op jit(solution)/shard_map/all_to_all | solution.py:73
  371.9 115.1 %all-gather.5.cloned.1.call-start = ((), (), s32[]{:S(2)}) async-start(), calls=%async_computation.7 | async-start | bytes 2088960 | tf_op jit(solution)/shard_map/all_gather | solution.py:54
  381.9 0.6 copy-start.10
  396.1 93.2 %copy-start.2 = (bf16[6144,128]{1,0:T(8,128)(2,1)S(1)}, bf16[6144,128]{1,0:T(8,128)(2,1)}, u32[]{:S(2)}) copy-start(bf16[6144,128]{1,0:T(8,128)(2,1)} %param.10) | copy-start | bytes 4718596
  396.1 93.2 %copy-start.6 = (f32[160,128]{1,0:T(8,128)S(1)}, f32[160,128]{1,0:T(8,128)}, u32[]{:S(2)}) copy-start(f32[160,128]{1,0:T(8,128)} %copy-done.5) | copy-start | bytes 245764
  396.1 93.2 %copy-start.9 = (f32[160,128]{1,0:T(8,128)S(1)}, f32[160,128]{1,0:T(8,128)}, u32[]{:S(2)}) copy-start(f32[160,128]{1,0:T(8,128)} %copy-done.8) | copy-start | bytes 245764
  396.8 324.0 %reduce-scatter.9.cloned.1.call-start = ((), (), s32[]{:S(2)}) async-start(), calls=%async_computation.9 | async-start | bytes 3342336
  489.3 1.4 copy-start.4
  489.3 1.4 copy-start.7
  494.1 282.8 %copy-start.11 = (f32[4,5,384]{2,1,0:T(8,128)S(1)}, f32[4,5,384]{2,1,0:T(8,128)}, u32[]{:S(2)}) copy-start(f32[4,5,384]{2,1,0:T(8,128)} %copy-done.10) | copy-start | bytes 92164
  722.6 55.1 %all-to-all-start.3 = ((bf16[32,5,384]{2,1,0:T(8,128)(2,1)}), bf16[32,5,384]{2,1,0:T(8,128)(2,1)S(1)}, u32[]{:S(2)}, u32[]{:S(2)}) async-start(bf16[32,5,384]{2,1,0:T(8,128)(2,1)} %all_to_all.36), calls=%async_computation.3 | async-start | bytes 393216 | tf_op jit(solution)/shard_map/all_to_all | solution.py:76
Sparse Core Ops, SparseCore 0:
  29.5 95.2 all-gather.2
  132.5 226.6 reduce-scatter.6
  396.9 90.0 all-gather.4
  494.3 226.4 reduce-scatter.8
where the time goes:
time: 792 us; the launch traced here: 785 us
  waiting for transfers between devices  649 us (82%)
  blocking collectives  76.2 us (10%)
  starting transfers between devices  22 us (3%)
  between operations  14 us (2%)
  local copies, waits for them, and re-layouts  12.2 us (2%)
  matrix products  10.6 us (1%)
    unnamed x6, waiting for transfers between devices  454 us
    all_gather x1, waiting for transfers between devices, body(): x_piece = lax.all_gather(x_recv, 'et', axis=1, tiled=True)  95.4 us
    all_gather x1, waiting for transfers between devices, body(): g_piece = lax.all_gather(g_recv, 'et', axis=1, tiled=True)  90.2 us
    psum x1, blocking collectives, body(): prob_grad = lax.psum(partial_grad, 'et')  43.3 us
    all_to_all x1, blocking collectives, body(): lax.all_to_all(x_send, 'de', split_axis=0, concat_axis=0, tiled=True)  19.5 us
  transfers between devices with their start and end apart: 6, of which 5 were waited for; matrix products, arithmetic and copies ran while one was open for 0% of the time, Pallas kernels for 0%

commit v1 on v0

v1 whole, which is shorter than its diff:
```python
import functools

import jax
import jax.numpy as jnp
from jax import lax
from jax.experimental import pallas as pl
from jax.experimental.pallas import tpu as pltpu
from jax.sharding import PartitionSpec as P

EXPERTS = 4
CAP = 5
SLOT = 8
Y_HI = 2
MESH = pl.DeviceIdType.MESH
F32 = jnp.float32
BF16 = jnp.bfloat16
HIGHEST = lax.Precision.HIGHEST


def dot(a, b, contract, precision=None):
    return lax.dot_general(
        a, b, ((contract[0], contract[1]), ((), ())), preferred_element_type=F32, precision=precision
    )


def fifth(p):
    return (p * 13) >> 6


def kernel(
    sizes,
    ids_ref,
    probs_ref,
    tok_ref,
    grad_ref,
    wg_hbm,
    wu_hbm,
    wd_hbm,
    mixed_ref,
    tgrad_ref,
    pgrad_ref,
    wgu,
    wdv,
    s1,
    r1,
    gb,
    acc_gu,
    acc_d,
    hid,
    dgu,
    tb,
    sr,
    rr,
    p2,
    s2,
    r2,
    pg,
    w_sem,
    s1_s,
    s1_r,
    p1_s,
    p1_r,
    ag_s,
    ag_r,
    sh_s,
    sh_r,
    st_s,
    st_r,
    rs_s,
    rs_r,
    p2_s,
    p2_r,
    s2_s,
    s2_r,
    pg_s,
    pg_r,
):
    nx, yl, n = sizes
    n2 = n // 2
    group = 2 * nx
    rows = group * CAP
    width = tok_ref.shape[1]
    hidden_units = wdv.shape[0]
    de, et = lax.axis_index("de"), lax.axis_index("et")
    c = lax.rem(de, 2)
    y_lo = lax.rem(lax.div(de, 2), yl)
    x = lax.div(de, 2 * yl)
    y_hi, z = lax.div(et, n), lax.rem(et, n)
    y = y_hi * yl + y_lo
    me = x * 2 + c
    b0 = jnp.where(c == 0, y, z)
    a0 = jnp.where(c == 0, z, y)

    def wrap(v, m):
        return lax.rem(v + m, m)

    def device(x_, y_, z_, c_):
        return ((x_ * yl + lax.rem(y_, yl)) * 2 + c_, lax.div(y_, yl) * n + z_)

    def at_ba(b_, a_):
        return device(x, jnp.where(c == 0, b_, a_), jnp.where(c == 0, a_, b_), c)

    def at_group(idx):
        return device(lax.div(idx, 2), y, z, lax.rem(idx, 2))

    sibling = device(x, y, z, 1 - c)
    onward = (at_ba(wrap(b0 + 1, n), a0), at_ba(wrap(b0 - 1, n), a0))
    sends = []

    def send(src, dst, s_sem, r_sem, to):
        copy = pltpu.make_async_remote_copy(
            src_ref=src, dst_ref=dst, send_sem=s_sem, recv_sem=r_sem, device_id=to, device_id_type=MESH
        )
        copy.start()
        sends.append(copy)

    def arrived(dst, sem):
        pltpu.make_async_copy(dst, dst, sem).wait()

    loads = (
        pltpu.make_async_copy(wg_hbm, wgu.at[:, pl.ds(0, hidden_units)], w_sem.at[0]),
        pltpu.make_async_copy(wu_hbm, wgu.at[:, pl.ds(hidden_units, hidden_units)], w_sem.at[1]),
        pltpu.make_async_copy(wd_hbm, wdv, w_sem.at[2]),
    )
    for load in loads:
        load.start()

    barrier = pltpu.get_barrier_semaphore()
    peers = [at_group(wrap(me + i, group)) for i in range(1, group)]
    for i in range(1, n):
        peers.append(device(x, y, wrap(z + i, n), c))
        peers.append(device(x, wrap(y + i, n), z, c))
        peers.append(device(x, wrap(y + yl, n), wrap(z + i, n), c))
    for peer in peers:
        pl.semaphore_signal(barrier, inc=1, device_id=peer, device_id_type=MESH)

    ids, probs = ids_ref[...], probs_ref[...]
    tokens = ids.shape[0]
    lane = lax.broadcasted_iota(jnp.int32, (tokens, 128), 1)
    row = lax.broadcasted_iota(jnp.int32, (tokens, 128), 0)
    named = jnp.where((ids[:, 0:1] == lane) | (ids[:, 1:2] == lane), 1.0, 0.0)
    rank = jnp.zeros((tokens, 128), F32)
    for t in range(tokens - 1):
        rank = rank + jnp.where(row > t, named[t : t + 1, :], 0.0)
    sel = []
    for j in range(2):
        e = ids[:, j : j + 1]
        rank_j = jnp.sum(jnp.where(lane == e, rank, 0.0), axis=1, keepdims=True)
        slot = e.astype(F32) * SLOT + rank_j
        sel.append(jnp.where(lane.astype(F32) == slot, 1.0, 0.0)[:, : nx * SLOT])
    tok_f, grad_f = tok_ref[...].astype(F32), grad_ref[...].astype(F32)
    first = ((0,), (0,))
    xs = dot(sel[0] + sel[1], tok_f, first, HIGHEST)
    gs = jnp.zeros_like(xs)
    for j in range(2):
        scaled = (probs[:, j : j + 1] * grad_f).astype(BF16).astype(F32)
        gs = gs + dot(sel[j], scaled, first, HIGHEST)
    for e in range(nx):
        block = slice(e * SLOT, (e + 1) * SLOT)
        s1[e] = jnp.concatenate([xs[block], gs[block]], axis=0).astype(BF16)

    pl.semaphore_wait(barrier, len(peers))

    for i in range(1, group):
        to = wrap(me + i, group)
        send(s1.at[lax.div(to, 2)], r1.at[me], s1_s.at[i], s1_r.at[i], at_group(to))
    r1[me] = s1[x]
    for i in range(1, group):
        arrived(r1.at[wrap(me - i, group)], s1_r.at[i])
    p = lax.broadcasted_iota(jnp.int32, (rows, group * 16), 0)
    col = lax.broadcasted_iota(jnp.int32, (rows, group * 16), 1)
    pick = jnp.where(col == p + 11 * fifth(p) + 8 * c, 1.0, 0.0).astype(BF16)
    staged = r1[...].reshape(group * 16, width)
    gb[c, b0, a0] = dot(pick, staged, ((1,), (0,))).astype(BF16)

    for i in range(1, n):
        send(gb.at[c, b0, a0], gb.at[c, b0, a0], p1_s.at[i], p1_r.at[a0], at_ba(b0, wrap(a0 + i, n)))

    def unit(b_, h):
        return gb.at[c, b_, pl.ds(h * n2, n2)]

    def share(b_, h):
        send(unit(b_, h), unit(b_, h), sh_s.at[b_, h], sh_r.at[b_, h], sibling)

    for h in range(2):
        for a_ in range(h * n2, (h + 1) * n2):

            @pl.when(a0 != a_)
            def _():
                arrived(gb.at[c, b0, a_], p1_r.at[a_])

        for d in range(2):
            send(unit(b0, h), unit(b0, h), ag_s.at[d, 0, h], ag_r.at[b0, h], onward[d])
        share(b0, h)
    for s in range(1, n2 + 1):
        for h in range(2):
            for d in range(2):
                if s == n2 and h != d:
                    continue
                b_ = wrap(b0 - s, n) if d == 0 else wrap(b0 + s, n)
                arrived(unit(b_, h), ag_r.at[b_, h])
                if s < n2 - 1 or (s == n2 - 1 and h == d):
                    send(unit(b_, h), unit(b_, h), ag_s.at[d, s, h], ag_r.at[b_, h], onward[d])
                share(b_, h)
    for b_ in range(n):
        for h in range(2):
            arrived(gb.at[1 - c, b_, pl.ds(h * n2, n2)], sh_r.at[b_, h])
    for load in loads:
        load.wait()

    acc_gu[...] = jnp.zeros_like(acc_gu)
    acc_d[...] = jnp.zeros_like(acc_d)

    @pl.loop(0, Y_HI * n)
    def _(q):
        hi, z_ = lax.div(q, n), lax.rem(q, n)
        span = pl.ds(pl.multiple_of(q * width, width), width)
        xq = jnp.concatenate([gb[0, hi * yl + k, z_] for k in range(yl)], axis=0)
        gq = jnp.concatenate([gb[1, z_, hi * yl + k] for k in range(yl)], axis=0)
        acc_gu[...] += dot(xq, wgu[span, :], ((1,), (0,)))
        acc_d[...] += dot(gq, wdv[:, span], ((1,), (1,)))

    gate, up, d_hidden = acc_gu[:, :hidden_units], acc_gu[:, hidden_units:], acc_d[...]
    sig = jax.nn.sigmoid(gate)
    hid[...] = (gate * sig * up).astype(BF16)
    dgu[:, :hidden_units] = (d_hidden * up * sig * (1.0 + gate * (1.0 - sig))).astype(BF16)
    dgu[:, hidden_units:] = (d_hidden * gate * sig).astype(BF16)

    def crossing(q, kind):
        hi, z_ = lax.div(q, n), lax.rem(q, n)
        part = pl.ds(hi * yl, yl)

        def copy(src, dst):
            return pltpu.make_async_remote_copy(
                src_ref=src,
                dst_ref=dst,
                send_sem=st_s.at[q],
                recv_sem=st_r.at[q],
                device_id=sibling,
                device_id_type=MESH,
            )

        if kind == 1:
            return copy(tb.at[1, z_, part], sr.at[z_, part])
        return copy(tb.at[0, part, z_], sr.at[part, z_])

    @pl.loop(0, Y_HI * n)
    def _(q):
        hi, z_ = lax.div(q, n), lax.rem(q, n)
        span = pl.ds(pl.multiple_of(q * width, width), width)
        yq = dot(hid[...], wdv[:, span], ((1,), (0,))).astype(BF16)
        xq = dot(dgu[...], wgu[span, :], ((1,), (1,))).astype(BF16)
        for k in range(yl):
            block = slice(k * rows, (k + 1) * rows)
            tb[0, hi * yl + k, z_] = yq[block]
            tb[1, z_, hi * yl + k] = xq[block]

        @pl.when(c == 0)
        def _():
            crossing(q, 1).start()

        @pl.when(c == 1)
        def _():
            crossing(q, 0).start()

    @pl.loop(0, Y_HI * n)
    def _(q):
        @pl.when(c == 0)
        def _():
            crossing(q, 1).wait_send()
            crossing(q, 0).wait_recv()

        @pl.when(c == 1)
        def _():
            crossing(q, 0).wait_send()
            crossing(q, 1).wait_recv()

    def half(h):
        return pl.ds(h * n2, n2)

    def own(t, h):
        return tb[c, t, half(h)].astype(F32) + sr[t, half(h)].astype(F32)

    for k in range(n2, 0, -1):
        for h in range(2):
            for d in range(2):
                if k == n2 and h != d:
                    continue
                t = wrap(b0 + k, n) if d == 0 else wrap(b0 - k, n)
                value = own(t, h)
                if k < n2 - 1 or (k == n2 - 1 and h == d):
                    arrived(rr.at[d, k, h], rs_r.at[d, k, h])
                    value = value + rr[d, k, h].astype(F32)
                tb[c, t, half(h)] = value.astype(BF16)
                send(
                    tb.at[c, t, half(h)],
                    rr.at[d, k - 1, h],
                    rs_s.at[d, k - 1, h],
                    rs_r.at[d, k - 1, h],
                    onward[d],
                )
    for h in range(2):
        value = own(b0, h)
        for d in range(2):
            arrived(rr.at[d, 0, h], rs_r.at[d, 0, h])
            value = value + rr[d, 0, h].astype(F32)
        tb[c, b0, half(h)] = value.astype(BF16)

    for i in range(1, n):
        to = wrap(a0 + i, n)
        send(tb.at[c, b0, to], p2.at[a0], p2_s.at[i], p2_r.at[i], at_ba(b0, to))
    total = tb[c, b0, a0].astype(F32)
    for i in range(1, n):
        a_ = wrap(a0 - i, n)
        arrived(p2.at[a_], p2_r.at[i])
        total = total + p2[a_].astype(F32)

    r = lax.broadcasted_iota(jnp.int32, (group * SLOT, rows), 0)
    p = lax.broadcasted_iota(jnp.int32, (group * SLOT, rows), 1)
    spread = jnp.where(r == p + 3 * fifth(p), 1.0, 0.0).astype(BF16)
    s2[...] = dot(spread, total.astype(BF16), ((1,), (0,))).reshape(group, SLOT, width).astype(BF16)
    for i in range(1, group):
        to = wrap(me + i, group)
        send(s2.at[to], r2.at[c, x], s2_s.at[i], s2_r.at[i], at_group(to))
    r2[c, x] = s2[me]
    for i in range(1, group):
        idx = wrap(me - i, group)
        arrived(r2.at[lax.rem(idx, 2), lax.div(idx, 2)], s2_r.at[i])

    last = ((1,), (0,))
    y_rows = r2[0].astype(F32).reshape(nx * SLOT, width)
    x_rows = r2[1].astype(F32).reshape(nx * SLOT, width)
    y_of = [dot(sel[j], y_rows, last, HIGHEST) for j in range(2)]
    part = jnp.zeros((tokens, 128), F32)
    for j in range(2):
        part = jnp.where(lane == j, jnp.sum(grad_f * y_of[j], axis=1, keepdims=True), part)
    pg[et] = part
    n_et = Y_HI * n
    for i in range(1, n_et):
        send(pg.at[et], pg.at[et], pg_s.at[i], pg_r.at[i], (de, wrap(et + i, n_et)))
    mixed_ref[...] = (probs[:, 0:1] * y_of[0] + probs[:, 1:2] * y_of[1]).astype(BF16)
    tgrad_ref[...] = dot(sel[0] + sel[1], x_rows, last, HIGHEST).astype(BF16)
    for i in range(1, n_et):
        arrived(pg.at[wrap(et - i, n_et)], pg_r.at[i])
    total = pg[0]
    for i in range(1, n_et):
        total = total + pg[i]
    pgrad_ref[...] = total[:, 0:2]
    for copy in sends:
        copy.wait_send()


def body(tokens, expert_ids, gate_probs, w_gate, w_up, w_down, out_grad):
    n_de, n_et = lax.axis_size("de"), lax.axis_size("et")
    nx = EXPERTS
    yl = n_de // (2 * nx)
    n = n_et // Y_HI
    n2 = n // 2
    group = 2 * nx
    rows = group * CAP
    count, width = tokens.shape
    depth, units = w_gate.shape
    slots = yl * rows
    vmem = pl.BlockSpec(memory_space=pltpu.VMEM)
    hbm = pl.BlockSpec(memory_space=pl.ANY)
    dma = pltpu.SemaphoreType.DMA
    return pl.pallas_call(
        functools.partial(kernel, (nx, yl, n)),
        out_shape=(
            jax.ShapeDtypeStruct((count, width), BF16),
            jax.ShapeDtypeStruct((count, width), BF16),
            jax.ShapeDtypeStruct(gate_probs.shape, F32),
        ),
        in_specs=[vmem] * 4 + [hbm] * 3,
        out_specs=(vmem, vmem, vmem),
        scratch_shapes=[
            pltpu.VMEM((depth, 2 * units), BF16),
            pltpu.VMEM((units, depth), BF16),
            pltpu.VMEM((nx, 16, width), BF16),
            pltpu.VMEM((group, 16, width), BF16),
            pltpu.VMEM((2, n, n, rows, width), BF16),
            pltpu.VMEM((slots, 2 * units), F32),
            pltpu.VMEM((slots, units), F32),
            pltpu.VMEM((slots, units), BF16),
            pltpu.VMEM((slots, 2 * units), BF16),
            pltpu.VMEM((2, n, n, rows, width), BF16),
            pltpu.VMEM((n, n, rows, width), BF16),
            pltpu.VMEM((2, n2, 2, n2, rows, width), BF16),
            pltpu.VMEM((n, rows, width), BF16),
            pltpu.VMEM((group, SLOT, width), BF16),
            pltpu.VMEM((2, nx, SLOT, width), BF16),
            pltpu.VMEM((n_et, count, 128), F32),
            dma((3,)),
            dma((group,)),
            dma((group,)),
            dma((n,)),
            dma((n,)),
            dma((2, n2, 2)),
            dma((n, 2)),
            dma((n, 2)),
            dma((n, 2)),
            dma((n_et,)),
            dma((n_et,)),
            dma((2, n2, 2)),
            dma((2, n2, 2)),
            dma((n,)),
            dma((n,)),
            dma((group,)),
            dma((group,)),
            dma((n_et,)),
            dma((n_et,)),
        ],
        compiler_params=pltpu.CompilerParams(
            collective_id=0, has_side_effects=True, vmem_limit_bytes=48 * 1024 * 1024
        ),
    )(expert_ids, gate_probs, tokens, out_grad, w_gate, w_up, w_down)


def solution(mesh):
    return jax.shard_map(
        body,
        mesh=mesh,
        in_specs=(
            P("de", "et"),
            P("de", None),
            P("de", None),
            P(None, ("de", "et")),
            P(None, ("de", "et")),
            P(("de", "et"), None),
            P("de", "et"),
        ),
        out_specs=(P("de", "et"), P("de", "et"), P("de", None)),
        check_vma=False,
    )
```

time: 792 us -> 104 us (0.13)
  waiting for transfers between devices: 649 us -> 0 us
  Pallas kernels: 0 us -> 94.4 us
  blocking collectives: 76.2 us -> 0 us
  starting transfers between devices: 22 us -> 0 us
  between operations: 14 us -> 0.65 us
  matrix products: 10.6 us -> 0 us
    unnamed x6 -> x0, waiting for transfers between devices: 454 us -> none
    all_gather x2 -> x0, waiting for transfers between devices: 186 us -> none  [the longest x1 95.4 us: body(): x_piece = lax.all_gather(x_recv, 'et', axis=1, tiled=True)]
    pallas_call x0 -> x1, Pallas kernels: none -> 94.4 us  [body(): pl.pallas_call(functools.partial(kernel, (nx, yl, n)), out_shape=(jax.Sha...]
    psum x1 -> x0, blocking collectives: 43.3 us -> none  [body(): prob_grad = lax.psum(partial_grad, 'et')]
    all_to_all x2 -> x0, blocking collectives: 32.8 us -> none  [the longest x1 19.5 us: body(): lax.all_to_all(x_send, 'de', split_axis=0, concat_axis=0, tiled=True)]
    all_to_all x2 -> x0, starting transfers between devices: 21.9 us -> none  [the longest x1 10.9 us: body(): lax.all_to_all(y_part.astype(jnp.bfloat16), 'de', split_axis=0, concat_ax...]
    dot_general x11 -> x0, matrix products: 10.6 us -> none  [the longest x1 2.8 us: body(): gate = jnp.dot(x_piece, w_gate, preferred_element_type=jnp.float32)]
    all_to_all x2 -> x0, waiting for transfers between devices: 9.83 us -> none  [the longest x1 9.82 us: body(): lax.all_to_all(y_part.astype(jnp.bfloat16), 'de', split_axis=0, concat_ax...]
  transfers between devices with their start and end apart: 6 -> 0, of which waited for: 5 -> 0; matrix products, arithmetic and copies ran while one was open for 0% -> 0% of each run, Pallas kernels for 0% -> 0%
where the time goes in v1:
time: 104 us
  Pallas kernels  94.4 us (91%)
  local copies, waits for them, and re-layouts  8.93 us (9%)
    pallas_call x1, Pallas kernels, body(): pl.pallas_call(functools.partial(kernel, (nx, yl, n)), out_shape=(jax.Sha...  94.4 us
    unnamed x14, local copies, waits for them, and re-layouts  8.3 us

profile of v1, /device:TPU:1, one launch (start us, length us, event | category | flops | bytes accessed | tf_op | source)
XLA Modules:
  0.0 103.9 jit_solution(14317436163792448756)
XLA Ops:
  0.6 0.8 copy.10.ids_ref
  1.4 0.8 copy.11.probs_ref
  2.1 0.0 copy-start
  2.1 1.4 %copy-done = bf16[6144,128]{1,0:T(8,128)(2,1)S(1)} copy-done((bf16[6144,128]{1,0:T(8,128)(2,1)S(1)}, bf16[6144,128]{1,0:T(8,128)(2,1)}, u32[]{:S(2)}) %copy-start) | copy-done | bytes 1572888
  3.5 0.0 copy-start.1
  3.5 1.4 %copy-done.1 = bf16[6144,128]{1,0:T(8,128)(2,1)S(1)} copy-done((bf16[6144,128]{1,0:T(8,128)(2,1)S(1)}, bf16[6144,128]{1,0:T(8,128)(2,1)}, u32[]{:S(2)}) %copy-start.1) | copy-done | bytes 1572888
  5.0 0.0 copy-start.2
  5.0 1.4 %copy-done.2 = bf16[128,6144]{1,0:T(8,128)(2,1)S(1)} copy-done((bf16[128,6144]{1,0:T(8,128)(2,1)S(1)}, bf16[128,6144]{1,0:T(8,128)(2,1)}, u32[]{:S(2)}) %copy-start.2) | copy-done | bytes 1572888
  6.4 0.0 copy-start.3
  6.4 0.7 copy-done.3
  7.1 0.0 copy-start.4
  7.1 0.7 copy-done.4
  7.7 94.4 %shard_map.94 = (bf16[8,384]{1,0:T(8,128)(2,1)S(1)}, bf16[8,384]{1,0:T(8,128)(2,1)S(1)}, f32[8,2]{1,0:T(8,128)S(1)}) custom-call(s32[8,2]{1,0:T(8,128)S(1)} %copy.10.ids_ref, f32[8,2]{1,0:T(8,128)S(1)} %copy.11.probs_ref, bf16[8,384]{1,0:T(8,128)(2,1)S(1)} %copy-done.3, bf16[8,384]{1,0:T(8,128)(2,1)S(1)} %copy-done.4, bf16[6144,128]{1,0:T(8,128)(2,1)S(1)} %copy-done, ...), custom_call_target="tpu_custom_call" | custom-call | tf_op jit(solution)/shard_map/pallas_call | solution.py:367
  102.1 0.6 copy.12
  102.7 0.6 copy.15
  103.3 0.6 copy.16
Async XLA Ops:
  2.1 1.4 %copy-start = (bf16[6144,128]{1,0:T(8,128)(2,1)S(1)}, bf16[6144,128]{1,0:T(8,128)(2,1)}, u32[]{:S(2)}) copy-start(bf16[6144,128]{1,0:T(8,128)(2,1)} %wg_hbm.1) | copy-start | bytes 4718596
  3.5 1.4 %copy-start.1 = (bf16[6144,128]{1,0:T(8,128)(2,1)S(1)}, bf16[6144,128]{1,0:T(8,128)(2,1)}, u32[]{:S(2)}) copy-start(bf16[6144,128]{1,0:T(8,128)(2,1)} %wu_hbm.1) | copy-start | bytes 4718596
  5.0 1.4 %copy-start.2 = (bf16[128,6144]{1,0:T(8,128)(2,1)S(1)}, bf16[128,6144]{1,0:T(8,128)(2,1)}, u32[]{:S(2)}) copy-start(bf16[128,6144]{1,0:T(8,128)(2,1)} %wd_hbm.1) | copy-start | bytes 4718596
  6.4 0.7 copy-start.3
  7.1 0.7 copy-start.4

commit v2 on v1

v2 whole, which is shorter than its diff:
```python
import functools

import jax
import jax.numpy as jnp
from jax import lax
from jax.experimental import pallas as pl
from jax.experimental.pallas import tpu as pltpu
from jax.sharding import PartitionSpec as P

EXPERTS = 4
CAP = 5
SLOT = 8
Y_HI = 2
PARTS = 4
MESH = pl.DeviceIdType.MESH
F32 = jnp.float32
BF16 = jnp.bfloat16
HIGHEST = lax.Precision.HIGHEST


def dot(a, b, contract, precision=None):
    return lax.dot_general(
        a, b, ((contract[0], contract[1]), ((), ())), preferred_element_type=F32, precision=precision
    )


def fifth(p):
    return (p * 13) >> 6


def kernel(
    sizes,
    ids_hbm,
    probs_hbm,
    tok_hbm,
    grad_hbm,
    wg_hbm,
    wu_hbm,
    wd_hbm,
    mixed_ref,
    tgrad_ref,
    pgrad_ref,
    ids_ref,
    probs_ref,
    tok_ref,
    grad_ref,
    wgu,
    wdv,
    s1,
    r1,
    gb,
    acc_gu,
    acc_d,
    hid,
    dgu,
    tb,
    sr,
    rr,
    p2,
    s2,
    r2,
    pg,
    in_sem,
    w_sem,
    s1_s,
    s1_r,
    p1_s,
    p1_r,
    ag_s,
    ag_r,
    sh_s,
    sh_r,
    st_s,
    st_r,
    rs_s,
    rs_r,
    p2_s,
    p2_r,
    s2_s,
    s2_r,
    pg_s,
    pg_r,
):
    nx, yl, n = sizes
    n2 = n // 2
    pa = n // PARTS
    group = 2 * nx
    rows = group * CAP
    tokens, width = tok_ref.shape
    units = wdv.shape[0]
    de, et = lax.axis_index("de"), lax.axis_index("et")
    c = lax.rem(de, 2)
    y_lo = lax.rem(lax.div(de, 2), yl)
    x = lax.div(de, 2 * yl)
    y_hi, z = lax.div(et, n), lax.rem(et, n)
    y = y_hi * yl + y_lo
    me = x * 2 + c
    b0 = jnp.where(c == 0, y, z)
    a0 = jnp.where(c == 0, z, y)

    def wrap(v, m):
        return lax.rem(v + m, m)

    def device(x_, y_, z_, c_):
        return ((x_ * yl + lax.rem(y_, yl)) * 2 + c_, lax.div(y_, yl) * n + z_)

    def at_ba(b_, a_):
        return device(x, jnp.where(c == 0, b_, a_), jnp.where(c == 0, a_, b_), c)

    def at_group(idx):
        return device(lax.div(idx, 2), y, z, lax.rem(idx, 2))

    sibling = device(x, y, z, 1 - c)
    onward = (at_ba(wrap(b0 + 1, n), a0), at_ba(wrap(b0 - 1, n), a0))
    sends = []

    def remote(src, dst, s_sem, r_sem, to):
        return pltpu.make_async_remote_copy(
            src_ref=src, dst_ref=dst, send_sem=s_sem, recv_sem=r_sem, device_id=to, device_id_type=MESH
        )

    def send(src, dst, s_sem, r_sem, to):
        copy = remote(src, dst, s_sem, r_sem, to)
        copy.start()
        sends.append(copy)

    def arrived(dst, sem):
        pltpu.make_async_copy(dst, dst, sem).wait()

    barrier = pltpu.get_barrier_semaphore()
    peers = [at_group(wrap(me + i, group)) for i in range(1, group)]
    for i in range(1, n):
        peers.append(device(x, y, wrap(z + i, n), c))
        peers.append(device(x, wrap(y + i, n), z, c))
        peers.append(device(x, wrap(y + yl, n), wrap(z + i, n), c))
    inputs = [
        pltpu.make_async_copy(src, dst, in_sem.at[i])
        for i, (src, dst) in enumerate(
            ((ids_hbm, ids_ref), (probs_hbm, probs_ref), (tok_hbm, tok_ref), (grad_hbm, grad_ref))
        )
    ]
    for copy in inputs:
        copy.start()
    for peer in peers:
        pl.semaphore_signal(barrier, inc=1, device_id=peer, device_id_type=MESH)
    for copy in inputs:
        copy.wait()

    ids = [ids_ref[j : j + 1, :] for j in range(2)]
    probs = [probs_ref[j : j + 1, :] for j in range(2)]
    expert = lax.broadcasted_iota(jnp.int32, (8, tokens), 0)
    named = jnp.where((expert == ids[0]) | (expert == ids[1]), 1.0, 0.0)
    before = lax.broadcasted_iota(jnp.int32, (tokens, tokens), 0)
    after = lax.broadcasted_iota(jnp.int32, (tokens, tokens), 1)
    last = ((1,), (0,))
    rank = dot(named, jnp.where(before < after, 1.0, 0.0), last, HIGHEST)
    slots = lax.broadcasted_iota(jnp.int32, (nx * SLOT, tokens), 0).astype(F32)
    place = []
    for j in range(2):
        rank_j = jnp.sum(jnp.where(expert == ids[j], rank, 0.0), axis=0, keepdims=True)
        place.append(jnp.where(slots == ids[j].astype(F32) * SLOT + rank_j, 1.0, 0.0))
    both = place[0] + place[1]
    weight = jnp.sum(place[0] * probs[0] + place[1] * probs[1], axis=1, keepdims=True)
    xs = dot(both, tok_ref[...].astype(F32), last, HIGHEST)
    raw = dot(both, grad_ref[...].astype(F32), last, HIGHEST)
    gs = weight * raw
    for e in range(nx):
        block = slice(e * SLOT, (e + 1) * SLOT)
        s1[e] = jnp.concatenate([xs[block], gs[block]], axis=0).astype(BF16)

    pl.semaphore_wait(barrier, len(peers))

    for i in range(1, group):
        to = wrap(me + i, group)
        send(s1.at[lax.div(to, 2)], r1.at[me], s1_s.at[i], s1_r.at[i], at_group(to))
    loads = (
        pltpu.make_async_copy(wg_hbm, wgu.at[:, pl.ds(0, units)], w_sem.at[0]),
        pltpu.make_async_copy(wu_hbm, wgu.at[:, pl.ds(units, units)], w_sem.at[1]),
        pltpu.make_async_copy(wd_hbm, wdv, w_sem.at[2]),
    )
    for load in loads:
        load.start()
    r1[me] = s1[x]
    acc_gu[...] = jnp.zeros_like(acc_gu)
    acc_d[...] = jnp.zeros_like(acc_d)
    p = lax.broadcasted_iota(jnp.int32, (rows, group * 16), 0)
    col = lax.broadcasted_iota(jnp.int32, (rows, group * 16), 1)
    pick = jnp.where(col == p + 11 * fifth(p) + 8 * c, 1.0, 0.0).astype(BF16)
    for i in range(1, group):
        arrived(r1.at[wrap(me - i, group)], s1_r.at[i])
    staged = r1[...].reshape(group * 16, width)
    gb[c, b0, a0] = dot(pick, staged, last).astype(BF16)

    for i in range(1, n):
        send(gb.at[c, b0, a0], gb.at[c, b0, a0], p1_s.at[i], p1_r.at[a0], at_ba(b0, wrap(a0 + i, n)))

    def part(h):
        return pl.ds(h * pa, pa)

    def takes(h, d):
        return (h < PARTS // 2) == (d == 0)

    def unit(b_, h):
        return gb.at[c, b_, part(h)]

    def share(b_, h):
        send(unit(b_, h), unit(b_, h), sh_s.at[b_, h], sh_r.at[b_, h], sibling)

    o0 = jnp.where(c == 0, z, y)

    def around(v, s):
        return [wrap(v + s, n)] if s in (0, n2) else [wrap(v + s, n), wrap(v - s, n)]

    def multiply(s):
        for o_ in around(o0, s):
            for h in range(PARTS):
                arrived(gb.at[1 - c, o_, part(h)], sh_r.at[o_, h])
        for z_ in around(z, s):
            total = acc_d[...]
            for hi in range(Y_HI):
                g = jnp.concatenate([gb[1, z_, hi * yl + k] for k in range(yl)], axis=0)
                span = pl.ds(pl.multiple_of((hi * n + z_) * width, width), width)
                total = total + dot(g, wdv[:, span], ((1,), (1,)))
            acc_d[...] = total
        for y_ in around(y, s):
            hi, lo = lax.div(y_, yl), lax.rem(y_, yl)
            v = jnp.concatenate([gb[0, y_, k] for k in range(n)], axis=1)
            span = pl.ds(pl.multiple_of(hi * (n * width), n * width), n * width)
            acc_gu[lo] += dot(v, wgu[span, :], last)

    for h in range(PARTS):
        for a_ in range(h * pa, (h + 1) * pa):

            @pl.when(a0 != a_)
            def _():
                arrived(gb.at[c, b0, a_], p1_r.at[a_])

        for d in range(2):
            send(unit(b0, h), unit(b0, h), ag_s.at[d, 0, h], ag_r.at[b0, h], onward[d])
        share(b0, h)
    for load in loads:
        load.wait()
    for s in range(1, n2 + 1):
        for h in range(PARTS):
            for d in range(2):
                if s == n2 and not takes(h, d):
                    continue
                b_ = wrap(b0 - s, n) if d == 0 else wrap(b0 + s, n)
                arrived(unit(b_, h), ag_r.at[b_, h])
                if s < n2 - 1 or (s == n2 - 1 and takes(h, d)):
                    send(unit(b_, h), unit(b_, h), ag_s.at[d, s, h], ag_r.at[b_, h], onward[d])
                share(b_, h)
        multiply(s - 1)
    multiply(n2)

    both_rows = acc_gu[...].reshape(yl * rows, 2 * units)
    gate, up, d_hidden = both_rows[:, :units], both_rows[:, units:], acc_d[...]
    sig = jax.nn.sigmoid(gate)
    hidden = (gate * sig * up).astype(BF16)
    for k in range(yl):
        hid[k] = hidden[k * rows : (k + 1) * rows]
    dgu[:, :units] = (d_hidden * up * sig * (1.0 + gate * (1.0 - sig))).astype(BF16)
    dgu[:, units:] = (d_hidden * gate * sig).astype(BF16)

    def terms(s):
        for z_ in around(z, s):
            for hi in range(Y_HI):
                span = pl.ds(pl.multiple_of((hi * n + z_) * width, width), width)
                v = dot(dgu[...], wgu[span, :], ((1,), (1,))).astype(BF16)
                for k in range(yl):
                    tb[1, z_, hi * yl + k] = v[k * rows : (k + 1) * rows]
        for y_ in around(y, s):
            hi, lo = lax.div(y_, yl), lax.rem(y_, yl)
            span = pl.ds(pl.multiple_of(hi * (n * width), n * width), n * width)
            v = dot(hid[lo], wdv[:, span], last).astype(BF16)
            for k in range(n):
                tb[0, y_, k] = v[:, k * width : (k + 1) * width]
        for o_ in around(o0, s):
            send(tb.at[1 - c, o_], sr.at[o_], st_s.at[o_], st_r.at[o_], sibling)

    def own(t, h):
        return tb[c, t, part(h)].astype(F32) + sr[t, part(h)].astype(F32)

    terms(n2)
    terms(n2 - 1)
    for k in range(n2, 0, -1):
        for t in around(b0, k):
            arrived(sr.at[t], st_r.at[t])
        for h in range(PARTS):
            for d in range(2):
                if k == n2 and not takes(h, d):
                    continue
                t = wrap(b0 + k, n) if d == 0 else wrap(b0 - k, n)
                value = own(t, h)
                if k < n2 - 1 or (k == n2 - 1 and takes(h, d)):
                    arrived(rr.at[d, k, h], rs_r.at[d, k, h])
                    value = value + rr[d, k, h].astype(F32)
                tb[c, t, part(h)] = value.astype(BF16)
                send(
                    tb.at[c, t, part(h)],
                    rr.at[d, k - 1, h],
                    rs_s.at[d, k - 1, h],
                    rs_r.at[d, k - 1, h],
                    onward[d],
                )
        if k >= 2:
            terms(k - 2)
    arrived(sr.at[b0], st_r.at[b0])

    def along(a_):
        return remote(tb.at[c, b0, a_], p2.at[a0], p2_s.at[a_], p2_r.at[a0], at_ba(b0, a_))

    for h in range(PARTS):
        value = own(b0, h)
        for d in range(2):
            arrived(rr.at[d, 0, h], rs_r.at[d, 0, h])
            value = value + rr[d, 0, h].astype(F32)
        tb[c, b0, part(h)] = value.astype(BF16)
        for a_ in range(h * pa, (h + 1) * pa):

            @pl.when(a0 != a_)
            def _():
                along(a_).start()

    total = tb[c, b0, a0].astype(F32)
    for i in range(1, n):
        a_ = wrap(a0 - i, n)
        arrived(p2.at[a_], p2_r.at[a_])
        total = total + p2[a_].astype(F32)

    r = lax.broadcasted_iota(jnp.int32, (group * SLOT, rows), 0)
    p = lax.broadcasted_iota(jnp.int32, (group * SLOT, rows), 1)
    spread = jnp.where(r == p + 3 * fifth(p), 1.0, 0.0).astype(BF16)
    s2[...] = dot(spread, total.astype(BF16), last).reshape(group, SLOT, width).astype(BF16)
    for i in range(1, group):
        to = wrap(me + i, group)
        send(s2.at[to], r2.at[c, x], s2_s.at[i], s2_r.at[i], at_group(to))
    r2[c, x] = s2[me]
    for i in range(1, group):
        idx = wrap(me - i, group)
        arrived(r2.at[lax.rem(idx, 2), lax.div(idx, 2)], s2_r.at[i])

    first = ((0,), (0,))
    y_rows = r2[0].astype(F32).reshape(nx * SLOT, width)
    x_rows = r2[1].astype(F32).reshape(nx * SLOT, width)
    score = jnp.sum(raw * y_rows, axis=1, keepdims=True)
    for j in range(2):
        pg[et, j : j + 1, 0:tokens] = jnp.sum(place[j] * score, axis=0, keepdims=True)
    n_et = Y_HI * n
    for i in range(1, n_et):
        send(pg.at[et], pg.at[et], pg_s.at[i], pg_r.at[i], (de, wrap(et + i, n_et)))
    mixed_ref[...] = dot(both, weight * y_rows, first, HIGHEST).astype(BF16)
    tgrad_ref[...] = dot(both, x_rows, first, HIGHEST).astype(BF16)
    for i in range(1, n_et):
        arrived(pg.at[wrap(et - i, n_et)], pg_r.at[i])
    sums = pg[0, 0:2, 0:tokens]
    for i in range(1, n_et):
        sums = sums + pg[i, 0:2, 0:tokens]
    pgrad_ref[...] = sums
    for copy in sends:
        copy.wait_send()
    for a_ in range(n):

        @pl.when(a0 != a_)
        def _():
            along(a_).wait_send()


def body(tokens, expert_ids, gate_probs, w_gate, w_up, w_down, out_grad):
    n_de, n_et = lax.axis_size("de"), lax.axis_size("et")
    nx = EXPERTS
    yl = n_de // (2 * nx)
    n = n_et // Y_HI
    n2 = n // 2
    pa = n // PARTS
    group = 2 * nx
    rows = group * CAP
    count, width = tokens.shape
    depth, units = w_gate.shape
    slots = yl * rows
    vmem = pl.BlockSpec(memory_space=pltpu.VMEM)
    hbm = pl.BlockSpec(memory_space=pltpu.HBM)
    dma = pltpu.SemaphoreType.DMA
    mixed, token_grad, prob_grad = pl.pallas_call(
        functools.partial(kernel, (nx, yl, n)),
        out_shape=(
            jax.ShapeDtypeStruct((count, width), BF16),
            jax.ShapeDtypeStruct((count, width), BF16),
            jax.ShapeDtypeStruct((2, count), F32),
        ),
        in_specs=[hbm] * 7,
        out_specs=(vmem, vmem, vmem),
        scratch_shapes=[
            pltpu.VMEM((2, count), jnp.int32),
            pltpu.VMEM((2, count), F32),
            pltpu.VMEM((count, width), BF16),
            pltpu.VMEM((count, width), BF16),
            pltpu.VMEM((depth, 2 * units), BF16),
            pltpu.VMEM((units, depth), BF16),
            pltpu.VMEM((nx, 16, width), BF16),
            pltpu.VMEM((group, 16, width), BF16),
            pltpu.VMEM((2, n, n, rows, width), BF16),
            pltpu.VMEM((yl, rows, 2 * units), F32),
            pltpu.VMEM((slots, units), F32),
            pltpu.VMEM((yl, rows, units), BF16),
            pltpu.VMEM((slots, 2 * units), BF16),
            pltpu.VMEM((2, n, n, rows, width), BF16),
            pltpu.VMEM((n, n, rows, width), BF16),
            pltpu.VMEM((2, n2, PARTS, pa, rows, width), BF16),
            pltpu.VMEM((n, rows, width), BF16),
            pltpu.VMEM((group, SLOT, width), BF16),
            pltpu.VMEM((2, nx, SLOT, width), BF16),
            pltpu.VMEM((n_et, 8, 128), F32),
            dma((4,)),
            dma((3,)),
            dma((group,)),
            dma((group,)),
            dma((n,)),
            dma((n,)),
            dma((2, n2, PARTS)),
            dma((n, PARTS)),
            dma((n, PARTS)),
            dma((n, PARTS)),
            dma((n,)),
            dma((n,)),
            dma((2, n2, PARTS)),
            dma((2, n2, PARTS)),
            dma((n,)),
            dma((n,)),
            dma((group,)),
            dma((group,)),
            dma((n_et,)),
            dma((n_et,)),
        ],
        compiler_params=pltpu.CompilerParams(
            collective_id=0, has_side_effects=True, vmem_limit_bytes=56 * 1024 * 1024
        ),
    )(expert_ids.T, gate_probs.T, tokens, out_grad, w_gate, w_up, w_down)
    return mixed, token_grad, prob_grad.T


def solution(mesh):
    return jax.shard_map(
        body,
        mesh=mesh,
        in_specs=(
            P("de", "et"),
            P("de", None),
            P("de", None),
            P(None, ("de", "et")),
            P(None, ("de", "et")),
            P(("de", "et"), None),
            P("de", "et"),
        ),
        out_specs=(P("de", "et"), P("de", "et"), P("de", None)),
        check_vma=False,
    )
```

time: 104 us -> 87.1 us (0.84)
  Pallas kernels: 94.4 us -> 82.4 us
  local copies, waits for them, and re-layouts: 8.93 us -> 3.8 us
    pallas_call x1, Pallas kernels: 94.4 us -> 82.4 us  [body(): pl.pallas_call(functools.partial(kernel, (nx, yl, n)), out_shape=(jax.Sha...]
    unnamed x14 -> x3, local copies, waits for them, and re-layouts: 8.3 us -> 3.8 us
where the time goes in v2:
time: 87.1 us; the launch traced here: 86.8 us
  Pallas kernels  82.4 us (95%)
  local copies, waits for them, and re-layouts  3.8 us (4%)
    pallas_call x1, Pallas kernels, body(): pl.pallas_call(functools.partial(kernel, (nx, yl, n)), out_shape=(jax.Sha...  82.4 us
    unnamed x3, local copies, waits for them, and re-layouts  3.8 us

profile of v2, /device:TPU:1, one launch (start us, length us, event | category | flops | bytes accessed | tf_op | source)
XLA Modules:
  0.0 86.8 jit_solution(2832539876475120317)
XLA Ops:
  0.6 82.4 %shard_map.94 = (bf16[8,384]{1,0:T(8,128)(2,1)}, bf16[8,384]{1,0:T(8,128)(2,1)}, f32[2,8]{1,0:T(2,128)}) custom-call(s32[2,8]{1,0:T(2,128)} %bitcast.3, f32[2,8]{1,0:T(2,128)} %bitcast.4, bf16[8,384]{1,0:T(8,128)(2,1)} %tok_hbm.1, bf16[8,384]{1,0:T(8,128)(2,1)} %grad_hbm.1, bf16[6144,128]{1,0:T(8,128)(2,1)} %wg_hbm.1, bf16[6144,128]{1,0:T(8,128)(2,1)} %wu_hbm.1, ...), custom_call_target="tpu_custom_call" | custom-call | tf_op jit(solution)/shard_map/pallas_call | solution.py:384
  83.0 1.3 %copy.13 = bf16[8,384]{1,0:T(8,128)(2,1)} copy(bf16[8,384]{1,0:T(8,128)(2,1)} %get-tuple-element.12) | data formatting | bytes 12288
  84.3 1.3 %copy.14 = bf16[8,384]{1,0:T(8,128)(2,1)} copy(bf16[8,384]{1,0:T(8,128)(2,1)} %get-tuple-element.13) | data formatting | bytes 12288
  85.6 1.2 %copy.15 = f32[8,2]{0,1:T(2,128)} copy(f32[8,2]{0,1:T(2,128)} %bitcast.5) | data formatting | bytes 128

commit v3 on v2

--- a/solution.py
+++ b/solution.py
@@ -59,7 +59,9 @@
     p2,
     s2,
     r2,
-    pg,
+    sc_z,
+    sc_y,
+    sc_c,
     in_sem,
     w_sem,
     s1_s,
@@ -78,8 +80,8 @@
     p2_r,
     s2_s,
     s2_r,
-    pg_s,
-    pg_r,
+    sc_s,
+    sc_r,
 ):
     nx, yl, n = sizes
     n2 = n // 2
@@ -112,17 +114,13 @@
 
     sibling = device(x, y, z, 1 - c)
     onward = (at_ba(wrap(b0 + 1, n), a0), at_ba(wrap(b0 - 1, n), a0))
-    sends = []
-
     def remote(src, dst, s_sem, r_sem, to):
         return pltpu.make_async_remote_copy(
             src_ref=src, dst_ref=dst, send_sem=s_sem, recv_sem=r_sem, device_id=to, device_id_type=MESH
         )
 
     def send(src, dst, s_sem, r_sem, to):
-        copy = remote(src, dst, s_sem, r_sem, to)
-        copy.start()
-        sends.append(copy)
+        remote(src, dst, s_sem, r_sem, to).start()
 
     def arrived(dst, sem):
         pltpu.make_async_copy(dst, dst, sem).wait()
@@ -132,7 +130,6 @@
     for i in range(1, n):
         peers.append(device(x, y, wrap(z + i, n), c))
         peers.append(device(x, wrap(y + i, n), z, c))
-        peers.append(device(x, wrap(y + yl, n), wrap(z + i, n), c))
     inputs = [
         pltpu.make_async_copy(src, dst, in_sem.at[i])
         for i, (src, dst) in enumerate(
@@ -153,17 +150,17 @@
     before = lax.broadcasted_iota(jnp.int32, (tokens, tokens), 0)
     after = lax.broadcasted_iota(jnp.int32, (tokens, tokens), 1)
     last = ((1,), (0,))
-    rank = dot(named, jnp.where(before < after, 1.0, 0.0), last, HIGHEST)
+    strict = jnp.where(before < after, 1.0, 0.0).astype(BF16)
+    rank = dot(named.astype(BF16), strict, last)
     slots = lax.broadcasted_iota(jnp.int32, (nx * SLOT, tokens), 0).astype(F32)
     place = []
     for j in range(2):
         rank_j = jnp.sum(jnp.where(expert == ids[j], rank, 0.0), axis=0, keepdims=True)
         place.append(jnp.where(slots == ids[j].astype(F32) * SLOT + rank_j, 1.0, 0.0))
-    both = place[0] + place[1]
+    both = (place[0] + place[1]).astype(BF16)
     weight = jnp.sum(place[0] * probs[0] + place[1] * probs[1], axis=1, keepdims=True)
-    xs = dot(both, tok_ref[...].astype(F32), last, HIGHEST)
-    raw = dot(both, grad_ref[...].astype(F32), last, HIGHEST)
-    gs = weight * raw
+    xs = dot(both, tok_ref[...], last)
+    gs = weight * dot(both, grad_ref[...], last)
     for e in range(nx):
         block = slice(e * SLOT, (e + 1) * SLOT)
         s1[e] = jnp.concatenate([xs[block], gs[block]], axis=0).astype(BF16)
@@ -172,7 +169,7 @@
 
     for i in range(1, group):
         to = wrap(me + i, group)
-        send(s1.at[lax.div(to, 2)], r1.at[me], s1_s.at[i], s1_r.at[i], at_group(to))
+        send(s1.at[lax.div(to, 2)], r1.at[me], s1_s, s1_r, at_group(to))
     loads = (
         pltpu.make_async_copy(wg_hbm, wgu.at[:, pl.ds(0, units)], w_sem.at[0]),
         pltpu.make_async_copy(wu_hbm, wgu.at[:, pl.ds(units, units)], w_sem.at[1]),
@@ -186,13 +183,16 @@
     p = lax.broadcasted_iota(jnp.int32, (rows, group * 16), 0)
     col = lax.broadcasted_iota(jnp.int32, (rows, group * 16), 1)
     pick = jnp.where(col == p + 11 * fifth(p) + 8 * c, 1.0, 0.0).astype(BF16)
-    for i in range(1, group):
-        arrived(r1.at[wrap(me - i, group)], s1_r.at[i])
+    eye = jnp.where(before == after, 1.0, 0.0)
+    turned = [dot(eye.astype(BF16), place[j].astype(BF16), ((1,), (1,))).astype(BF16) for j in range(2)]
+    share_of = [jnp.sum(eye * probs[j], axis=1, keepdims=True) for j in range(2)]
+    inverse = jnp.where(weight > 0.0, 1.0 / jnp.where(weight > 0.0, weight, 1.0), 0.0)
+    arrived(r1.at[pl.ds(0, group - 1)], s1_r)
     staged = r1[...].reshape(group * 16, width)
     gb[c, b0, a0] = dot(pick, staged, last).astype(BF16)
 
     for i in range(1, n):
-        send(gb.at[c, b0, a0], gb.at[c, b0, a0], p1_s.at[i], p1_r.at[a0], at_ba(b0, wrap(a0 + i, n)))
+        send(gb.at[c, b0, a0], gb.at[c, b0, a0], p1_s, p1_r.at[a0], at_ba(b0, wrap(a0 + i, n)))
 
     def part(h):
         return pl.ds(h * pa, pa)
@@ -204,7 +204,7 @@
         return gb.at[c, b_, part(h)]
 
     def share(b_, h):
-        send(unit(b_, h), unit(b_, h), sh_s.at[b_, h], sh_r.at[b_, h], sibling)
+        send(unit(b_, h), unit(b_, h), sh_s, sh_r.at[b_], sibling)
 
     o0 = jnp.where(c == 0, z, y)
 
@@ -213,8 +213,7 @@
 
     def multiply(s):
         for o_ in around(o0, s):
-            for h in range(PARTS):
-                arrived(gb.at[1 - c, o_, part(h)], sh_r.at[o_, h])
+            arrived(gb.at[1 - c, o_], sh_r.at[o_])
         for z_ in around(z, s):
             total = acc_d[...]
             for hi in range(Y_HI):
@@ -236,7 +235,7 @@
                 arrived(gb.at[c, b0, a_], p1_r.at[a_])
 
         for d in range(2):
-            send(unit(b0, h), unit(b0, h), ag_s.at[d, 0, h], ag_r.at[b0, h], onward[d])
+            send(unit(b0, h), unit(b0, h), ag_s, ag_r.at[b0, h], onward[d])
         share(b0, h)
     for load in loads:
         load.wait()
@@ -248,7 +247,7 @@
                 b_ = wrap(b0 - s, n) if d == 0 else wrap(b0 + s, n)
                 arrived(unit(b_, h), ag_r.at[b_, h])
                 if s < n2 - 1 or (s == n2 - 1 and takes(h, d)):
-                    send(unit(b_, h), unit(b_, h), ag_s.at[d, s, h], ag_r.at[b_, h], onward[d])
+                    send(unit(b_, h), unit(b_, h), ag_s, ag_r.at[b_, h], onward[d])
                 share(b_, h)
         multiply(s - 1)
     multiply(n2)
@@ -261,6 +260,22 @@
         hid[k] = hidden[k * rows : (k + 1) * rows]
     dgu[:, :units] = (d_hidden * up * sig * (1.0 + gate * (1.0 - sig))).astype(BF16)
     dgu[:, units:] = (d_hidden * gate * sig).astype(BF16)
+    ones = jnp.ones((8, units), F32)
+    sc_z[z, :, 0 : yl * rows] = dot(ones, hidden.astype(F32) * d_hidden, ((1,), (1,)), HIGHEST)
+
+    def score_step(stage):
+        if stage == 0:
+            for i in range(1, n):
+                send(sc_z.at[z], sc_z.at[z], sc_s.at[0], sc_r.at[0], device(x, y, wrap(z + i, n), c))
+        if stage == 1:
+            arrived(sc_z.at[pl.ds(0, n - 1)], sc_r.at[0])
+            sc_y[y] = jnp.sum(sc_z[...], axis=0)
+            for i in range(1, n):
+                send(sc_y.at[y], sc_y.at[y], sc_s.at[1], sc_r.at[1], device(x, wrap(y + i, n), z, c))
+        if stage == 2:
+            arrived(sc_y.at[pl.ds(0, n - 1)], sc_r.at[1])
+            sc_c[c] = jnp.sum(sc_y[...], axis=0)
+            send(sc_c.at[c], sc_c.at[c], sc_s.at[2], sc_r.at[2], sibling)
 
     def terms(s):
         for z_ in around(z, s):
@@ -276,13 +291,14 @@
             for k in range(n):
                 tb[0, y_, k] = v[:, k * width : (k + 1) * width]
         for o_ in around(o0, s):
-            send(tb.at[1 - c, o_], sr.at[o_], st_s.at[o_], st_r.at[o_], sibling)
+            send(tb.at[1 - c, o_], sr.at[o_], st_s, st_r.at[o_], sibling)
 
     def own(t, h):
         return tb[c, t, part(h)].astype(F32) + sr[t, part(h)].astype(F32)
 
     terms(n2)
     terms(n2 - 1)
+    score_step(0)
     for k in range(n2, 0, -1):
         for t in around(b0, k):
             arrived(sr.at[t], st_r.at[t])
@@ -299,16 +315,17 @@
                 send(
                     tb.at[c, t, part(h)],
                     rr.at[d, k - 1, h],
-                    rs_s.at[d, k - 1, h],
+                    rs_s,
                     rs_r.at[d, k - 1, h],
                     onward[d],
                 )
         if k >= 2:
             terms(k - 2)
+        score_step(n2 + 1 - k)
     arrived(sr.at[b0], st_r.at[b0])
 
     def along(a_):
-        return remote(tb.at[c, b0, a_], p2.at[a0], p2_s.at[a_], p2_r.at[a0], at_ba(b0, a_))
+        return remote(tb.at[c, b0, a_], p2.at[a0], p2_s, p2_r, at_ba(b0, a_))
 
     for h in range(PARTS):
         value = own(b0, h)
@@ -322,48 +339,55 @@
             def _():
                 along(a_).start()
 
+    arrived(sc_c.at[0], sc_r.at[2])
+    scores = sc_c[0, 0:1, :] + sc_c[1, 0:1, :]
+    lane = lax.broadcasted_iota(jnp.int32, (rows, scores.shape[1]), 1)
+    row = lax.broadcasted_iota(jnp.int32, (rows, scores.shape[1]), 0)
+    score = jnp.sum(jnp.where(lane == row + y_lo * rows, scores, 0.0), axis=1, keepdims=True)
+    high = score.astype(BF16).astype(F32)
+    lane = lane[:, :128]
+    ending = jnp.where(lane == 0, high, jnp.where(lane == 1, score - high, 0.0)).astype(BF16)
+    arrived(p2.at[pl.ds(0, n - 1)], p2_r)
     total = tb[c, b0, a0].astype(F32)
     for i in range(1, n):
-        a_ = wrap(a0 - i, n)
-        arrived(p2.at[a_], p2_r.at[a_])
-        total = total + p2[a_].astype(F32)
+        total = total + p2[wrap(a0 - i, n)].astype(F32)
 
     r = lax.broadcasted_iota(jnp.int32, (group * SLOT, rows), 0)
     p = lax.broadcasted_iota(jnp.int32, (group * SLOT, rows), 1)
     spread = jnp.where(r == p + 3 * fifth(p), 1.0, 0.0).astype(BF16)
-    s2[...] = dot(spread, total.astype(BF16), last).reshape(group, SLOT, width).astype(BF16)
+    full = jnp.concatenate([total.astype(BF16), ending], axis=1)
+    s2[...] = dot(spread, full, last).reshape(group, SLOT, width + 128).astype(BF16)
     for i in range(1, group):
         to = wrap(me + i, group)
-        send(s2.at[to], r2.at[c, x], s2_s.at[i], s2_r.at[i], at_group(to))
+        send(s2.at[to], r2.at[c, x], s2_s, s2_r, at_group(to))
     r2[c, x] = s2[me]
-    for i in range(1, group):
-        idx = wrap(me - i, group)
-        arrived(r2.at[lax.rem(idx, 2), lax.div(idx, 2)], s2_r.at[i])
-
-    first = ((0,), (0,))
-    y_rows = r2[0].astype(F32).reshape(nx * SLOT, width)
-    x_rows = r2[1].astype(F32).reshape(nx * SLOT, width)
-    score = jnp.sum(raw * y_rows, axis=1, keepdims=True)
+    arrived(s2.at[pl.ds(0, group - 1)], s2_r)
+
+    y_rows = r2[0].astype(F32).reshape(nx * SLOT, width + 128)
+    x_rows = r2[1].astype(F32).reshape(nx * SLOT, width + 128)
+    score = (y_rows[:, width : width + 1] + y_rows[:, width + 1 : width + 2]) * inverse
     for j in range(2):
-        pg[et, j : j + 1, 0:tokens] = jnp.sum(place[j] * score, axis=0, keepdims=True)
-    n_et = Y_HI * n
-    for i in range(1, n_et):
-        send(pg.at[et], pg.at[et], pg_s.at[i], pg_r.at[i], (de, wrap(et + i, n_et)))
-    mixed_ref[...] = dot(both, weight * y_rows, first, HIGHEST).astype(BF16)
-    tgrad_ref[...] = dot(both, x_rows, first, HIGHEST).astype(BF16)
-    for i in range(1, n_et):
-        arrived(pg.at[wrap(et - i, n_et)], pg_r.at[i])
-    sums = pg[0, 0:2, 0:tokens]
-    for i in range(1, n_et):
-        sums = sums + pg[i, 0:2, 0:tokens]
-    pgrad_ref[...] = sums
-    for copy in sends:
-        copy.wait_send()
-    for a_ in range(n):
-
-        @pl.when(a0 != a_)
-        def _():
-            along(a_).wait_send()
+        pgrad_ref[j : j + 1, :] = jnp.sum(place[j] * score, axis=0, keepdims=True)
+    y_rows = y_rows[:, :width].astype(BF16)
+    x_rows = x_rows[:, :width].astype(BF16)
+    mixed_ref[...] = (
+        share_of[0] * dot(turned[0], y_rows, last) + share_of[1] * dot(turned[1], y_rows, last)
+    ).astype(BF16)
+    tgrad_ref[...] = dot(turned[0] + turned[1], x_rows, last).astype(BF16)
+    for done, sem in (
+        (r1.at[pl.ds(0, group - 1)], s1_s),
+        (gb.at[0, 0, pl.ds(0, n - 1)], p1_s),
+        (gb.at[0, pl.ds(0, n - 1)], ag_s),
+        (gb.at[0], sh_s),
+        (gb.at[0], st_s),
+        (gb.at[0, pl.ds(0, n - 1)], rs_s),
+        (gb.at[0, 0, pl.ds(0, n - 1)], p2_s),
+        (s2.at[pl.ds(0, group - 1)], s2_s),
+        (sc_z.at[pl.ds(0, n - 1)], sc_s.at[0]),
+        (sc_y.at[pl.ds(0, n - 1)], sc_s.at[1]),
+        (sc_c.at[0], sc_s.at[2]),
+    ):
+        arrived(done, sem)
 
 
 def body(tokens, expert_ids, gate_probs, w_gate, w_up, w_down, out_grad):
@@ -378,6 +402,7 @@
     count, width = tokens.shape
     depth, units = w_gate.shape
     slots = yl * rows
+    lanes = pl.cdiv(slots, 128) * 128
     vmem = pl.BlockSpec(memory_space=pltpu.VMEM)
     hbm = pl.BlockSpec(memory_space=pltpu.HBM)
     dma = pltpu.SemaphoreType.DMA
@@ -408,29 +433,31 @@
             pltpu.VMEM((n, n, rows, width), BF16),
             pltpu.VMEM((2, n2, PARTS, pa, rows, width), BF16),
             pltpu.VMEM((n, rows, width), BF16),
-            pltpu.VMEM((group, SLOT, width), BF16),
-            pltpu.VMEM((2, nx, SLOT, width), BF16),
-            pltpu.VMEM((n_et, 8, 128), F32),
+            pltpu.VMEM((group, SLOT, width + 128), BF16),
+            pltpu.VMEM((2, nx, SLOT, width + 128), BF16),
+            pltpu.VMEM((n, 8, lanes), F32),
+            pltpu.VMEM((n, 8, lanes), F32),
+            pltpu.VMEM((2, 8, lanes), F32),
             dma((4,)),
             dma((3,)),
-            dma((group,)),
-            dma((group,)),
+            dma(()),
+            dma(()),
+            dma(()),
             dma((n,)),
+            dma(()),
+            dma((n, PARTS)),
+            dma(()),
             dma((n,)),
+            dma(()),
+            dma((n,)),
+            dma(()),
             dma((2, n2, PARTS)),
-            dma((n, PARTS)),
-            dma((n, PARTS)),
-            dma((n, PARTS)),
-            dma((n,)),
-            dma((n,)),
-            dma((2, n2, PARTS)),
-            dma((2, n2, PARTS)),
-            dma((n,)),
-            dma((n,)),
-            dma((group,)),
-            dma((group,)),
-            dma((n_et,)),
-            dma((n_et,)),
+            dma(()),
+            dma(()),
+            dma(()),
+            dma(()),
+            dma((3,)),
+            dma((3,)),
         ],
         compiler_params=pltpu.CompilerParams(
             collective_id=0, has_side_effects=True, vmem_limit_bytes=56 * 1024 * 1024

time: 87.1 us -> 78.2 us (0.90)
  Pallas kernels: 82.4 us -> 73.4 us
    pallas_call x1, Pallas kernels: 82.4 us -> 73.4 us  [body(): pl.pallas_call(functools.partial(kernel, (nx, yl, n)), out_shape=(jax.Sha...]
where the time goes in v3:
time: 78.2 us; the launch traced here: 77.9 us
  Pallas kernels  73.4 us (94%)
  local copies, waits for them, and re-layouts  3.8 us (5%)
    pallas_call x1, Pallas kernels, body(): pl.pallas_call(functools.partial(kernel, (nx, yl, n)), out_shape=(jax.Sha...  73.4 us
    unnamed x3, local copies, waits for them, and re-layouts  3.8 us

profile of v3, /device:TPU:1, one launch (start us, length us, event | category | flops | bytes accessed | tf_op | source)
XLA Modules:
  0.0 77.9 jit_solution(1255242175790130564)
XLA Ops:
  0.6 73.4 %shard_map.94 = (bf16[8,384]{1,0:T(8,128)(2,1)}, bf16[8,384]{1,0:T(8,128)(2,1)}, f32[2,8]{1,0:T(2,128)}) custom-call(s32[2,8]{1,0:T(2,128)} %bitcast.3, f32[2,8]{1,0:T(2,128)} %bitcast.4, bf16[8,384]{1,0:T(8,128)(2,1)} %tok_hbm.1, bf16[8,384]{1,0:T(8,128)(2,1)} %grad_hbm.1, bf16[6144,128]{1,0:T(8,128)(2,1)} %wg_hbm.1, bf16[6144,128]{1,0:T(8,128)(2,1)} %wu_hbm.1, ...), custom_call_target="tpu_custom_call" | custom-call | tf_op jit(solution)/shard_map/pallas_call | solution.py:409
  74.1 1.3 %copy.13 = bf16[8,384]{1,0:T(8,128)(2,1)} copy(bf16[8,384]{1,0:T(8,128)(2,1)} %get-tuple-element.12) | data formatting | bytes 12288
  75.3 1.3 %copy.14 = bf16[8,384]{1,0:T(8,128)(2,1)} copy(bf16[8,384]{1,0:T(8,128)(2,1)} %get-tuple-element.13) | data formatting | bytes 12288
  76.6 1.2 %copy.15 = f32[8,2]{0,1:T(2,128)} copy(f32[8,2]{0,1:T(2,128)} %bitcast.5) | data formatting | bytes 128

commit v4 on v3

--- a/solution.py
+++ b/solution.py
@@ -11,7 +11,7 @@
 CAP = 5
 SLOT = 8
 Y_HI = 2
-PARTS = 4
+PARTS = 8
 MESH = pl.DeviceIdType.MESH
 F32 = jnp.float32
 BF16 = jnp.bfloat16
@@ -183,10 +183,6 @@
     p = lax.broadcasted_iota(jnp.int32, (rows, group * 16), 0)
     col = lax.broadcasted_iota(jnp.int32, (rows, group * 16), 1)
     pick = jnp.where(col == p + 11 * fifth(p) + 8 * c, 1.0, 0.0).astype(BF16)
-    eye = jnp.where(before == after, 1.0, 0.0)
-    turned = [dot(eye.astype(BF16), place[j].astype(BF16), ((1,), (1,))).astype(BF16) for j in range(2)]
-    share_of = [jnp.sum(eye * probs[j], axis=1, keepdims=True) for j in range(2)]
-    inverse = jnp.where(weight > 0.0, 1.0 / jnp.where(weight > 0.0, weight, 1.0), 0.0)
     arrived(r1.at[pl.ds(0, group - 1)], s1_r)
     staged = r1[...].reshape(group * 16, width)
     gb[c, b0, a0] = dot(pick, staged, last).astype(BF16)
@@ -260,11 +256,11 @@
         hid[k] = hidden[k * rows : (k + 1) * rows]
     dgu[:, :units] = (d_hidden * up * sig * (1.0 + gate * (1.0 - sig))).astype(BF16)
     dgu[:, units:] = (d_hidden * gate * sig).astype(BF16)
-    ones = jnp.ones((8, units), F32)
-    sc_z[z, :, 0 : yl * rows] = dot(ones, hidden.astype(F32) * d_hidden, ((1,), (1,)), HIGHEST)
 
     def score_step(stage):
         if stage == 0:
+            ones = jnp.ones((8, units), F32)
+            sc_z[z, :, 0 : yl * rows] = dot(ones, hidden.astype(F32) * d_hidden, ((1,), (1,)), HIGHEST)
             for i in range(1, n):
                 send(sc_z.at[z], sc_z.at[z], sc_s.at[0], sc_r.at[0], device(x, y, wrap(z + i, n), c))
         if stage == 1:
@@ -361,6 +357,10 @@
         to = wrap(me + i, group)
         send(s2.at[to], r2.at[c, x], s2_s, s2_r, at_group(to))
     r2[c, x] = s2[me]
+    eye = jnp.where(before == after, 1.0, 0.0)
+    turned = [dot(eye.astype(BF16), place[j].astype(BF16), ((1,), (1,))).astype(BF16) for j in range(2)]
+    share_of = [jnp.sum(eye * probs[j], axis=1, keepdims=True) for j in range(2)]
+    inverse = jnp.where(weight > 0.0, 1.0 / jnp.where(weight > 0.0, weight, 1.0), 0.0)
     arrived(s2.at[pl.ds(0, group - 1)], s2_r)
 
     y_rows = r2[0].astype(F32).reshape(nx * SLOT, width + 128)
@@ -388,6 +388,17 @@
         (sc_c.at[0], sc_s.at[2]),
     ):
         arrived(done, sem)
+
+
+def settle(mixed_in, tgrad_in, pgrad_in, mixed_ref, tgrad_ref, pgrad_ref, sem):
+    copies = [
+        pltpu.make_async_copy(src, dst, sem.at[i])
+        for i, (src, dst) in enumerate(((mixed_in, mixed_ref), (tgrad_in, tgrad_ref), (pgrad_in, pgrad_ref)))
+    ]
+    for copy in copies:
+        copy.start()
+    for copy in copies:
+        copy.wait()
 
 
 def body(tokens, expert_ids, gate_probs, w_gate, w_up, w_down, out_grad):
@@ -463,6 +474,14 @@
             collective_id=0, has_side_effects=True, vmem_limit_bytes=56 * 1024 * 1024
         ),
     )(expert_ids.T, gate_probs.T, tokens, out_grad, w_gate, w_up, w_down)
+    mixed, token_grad, prob_grad = pl.pallas_call(
+        settle,
+        out_shape=tuple(jax.ShapeDtypeStruct(v.shape, v.dtype) for v in (mixed, token_grad, prob_grad)),
+        in_specs=[hbm] * 3,
+        out_specs=(hbm, hbm, hbm),
+        scratch_shapes=[dma((3,))],
+        compiler_params=pltpu.CompilerParams(vmem_limit_bytes=56 * 1024 * 1024),
+    )(mixed, token_grad, prob_grad)
     return mixed, token_grad, prob_grad.T
 
 

time: 78.2 us -> 74.9 us (0.958)
  local copies, waits for them, and re-layouts: 3.8 us -> 0 us
    unnamed x3 -> x0, local copies, waits for them, and re-layouts: 3.8 us -> none
    pallas_call x0 -> x1, Pallas kernels: none -> 1.53 us  [body(): pl.pallas_call(settle, out_shape=tuple((jax.ShapeDtypeStruct(v.shape, v.d...]
    pallas_call x1, Pallas kernels: 73.4 us -> 72.6 us  [body(): pl.pallas_call(functools.partial(kernel, (nx, yl, n)), out_shape=(jax.Sha...]
where the time goes in v4:
time: 74.9 us; the launch traced here: 74.7 us
  Pallas kernels  74.1 us (99%)
    pallas_call x1, Pallas kernels, body(): pl.pallas_call(functools.partial(kernel, (nx, yl, n)), out_shape=(jax.Sha...  72.6 us
    pallas_call x1, Pallas kernels, body(): pl.pallas_call(settle, out_shape=tuple((jax.ShapeDtypeStruct(v.shape, v.d...  1.53 us

profile of v4, /device:TPU:1, one launch (start us, length us, event | category | flops | bytes accessed | tf_op | source)
XLA Modules:
  0.0 74.7 jit_solution(5215918139491232576)
XLA Ops:
  0.6 72.6 %shard_map.94 = (bf16[8,384]{1,0:T(8,128)(2,1)}, bf16[8,384]{1,0:T(8,128)(2,1)}, f32[2,8]{1,0:T(2,128)}) custom-call(s32[2,8]{1,0:T(2,128)} %bitcast.3, f32[2,8]{1,0:T(2,128)} %bitcast.4, bf16[8,384]{1,0:T(8,128)(2,1)} %tok_hbm.1, bf16[8,384]{1,0:T(8,128)(2,1)} %grad_hbm.1, bf16[6144,128]{1,0:T(8,128)(2,1)} %wg_hbm.1, bf16[6144,128]{1,0:T(8,128)(2,1)} %wu_hbm.1, ...), custom_call_target="tpu_custom_call" | custom-call | tf_op jit(solution)/shard_map/pallas_call | solution.py:420
  73.2 1.5 %shard_map.95 = (bf16[8,384]{1,0:T(8,128)(2,1)}, bf16[8,384]{1,0:T(8,128)(2,1)}, f32[2,8]{1,0:T(2,128)}) custom-call(bf16[8,384]{1,0:T(8,128)(2,1)} %get-tuple-element.9.mixed_in, bf16[8,384]{1,0:T(8,128)(2,1)} %get-tuple-element.10.tgrad_in, f32[2,8]{1,0:T(2,128)} %get-tuple-element.11.pgrad_in), custom_call_target="tpu_custom_call" | custom-call | tf_op jit(solution)/shard_map/pallas_call | solution.py:477

commit v5 on v4

--- a/solution.py
+++ b/solution.py
@@ -11,7 +11,6 @@
 CAP = 5
 SLOT = 8
 Y_HI = 2
-PARTS = 8
 MESH = pl.DeviceIdType.MESH
 F32 = jnp.float32
 BF16 = jnp.bfloat16
@@ -85,7 +84,7 @@
 ):
     nx, yl, n = sizes
     n2 = n // 2
-    pa = n // PARTS
+    pa = 1
     group = 2 * nx
     rows = group * CAP
     tokens, width = tok_ref.shape
@@ -190,14 +189,17 @@
     for i in range(1, n):
         send(gb.at[c, b0, a0], gb.at[c, b0, a0], p1_s, p1_r.at[a0], at_ba(b0, wrap(a0 + i, n)))
 
+    offsets = [0] + [v for i in range(1, n2) for v in (i, -i)] + [n2]
+    pieces = [wrap(a0 + v, n) if v else a0 for v in offsets]
+
     def part(h):
         return pl.ds(h * pa, pa)
 
     def takes(h, d):
-        return (h < PARTS // 2) == (d == 0)
+        return (h < n // 2) == (d == 0)
 
     def unit(b_, h):
-        return gb.at[c, b_, part(h)]
+        return gb.at[c, b_, pieces[h]]
 
     def share(b_, h):
         send(unit(b_, h), unit(b_, h), sh_s, sh_r.at[b_], sibling)
@@ -223,20 +225,16 @@
             span = pl.ds(pl.multiple_of(hi * (n * width), n * width), n * width)
             acc_gu[lo] += dot(v, wgu[span, :], last)
 
-    for h in range(PARTS):
-        for a_ in range(h * pa, (h + 1) * pa):
-
-            @pl.when(a0 != a_)
-            def _():
-                arrived(gb.at[c, b0, a_], p1_r.at[a_])
-
+    for h in range(n):
+        if h:
+            arrived(unit(b0, h), p1_r.at[pieces[h]])
         for d in range(2):
             send(unit(b0, h), unit(b0, h), ag_s, ag_r.at[b0, h], onward[d])
         share(b0, h)
     for load in loads:
         load.wait()
     for s in range(1, n2 + 1):
-        for h in range(PARTS):
+        for h in range(n):
             for d in range(2):
                 if s == n2 and not takes(h, d):
                     continue
@@ -298,7 +296,7 @@
     for k in range(n2, 0, -1):
         for t in around(b0, k):
             arrived(sr.at[t], st_r.at[t])
-        for h in range(PARTS):
+        for h in range(n):
             for d in range(2):
                 if k == n2 and not takes(h, d):
                     continue
@@ -323,7 +321,7 @@
     def along(a_):
         return remote(tb.at[c, b0, a_], p2.at[a0], p2_s, p2_r, at_ba(b0, a_))
 
-    for h in range(PARTS):
+    for h in range(n):
         value = own(b0, h)
         for d in range(2):
             arrived(rr.at[d, 0, h], rs_r.at[d, 0, h])
@@ -407,7 +405,7 @@
     yl = n_de // (2 * nx)
     n = n_et // Y_HI
     n2 = n // 2
-    pa = n // PARTS
+    pa = 1
     group = 2 * nx
     rows = group * CAP
     count, width = tokens.shape
@@ -442,7 +440,7 @@
             pltpu.VMEM((slots, 2 * units), BF16),
             pltpu.VMEM((2, n, n, rows, width), BF16),
             pltpu.VMEM((n, n, rows, width), BF16),
-            pltpu.VMEM((2, n2, PARTS, pa, rows, width), BF16),
+            pltpu.VMEM((2, n2, n, pa, rows, width), BF16),
             pltpu.VMEM((n, rows, width), BF16),
             pltpu.VMEM((group, SLOT, width + 128), BF16),
             pltpu.VMEM((2, nx, SLOT, width + 128), BF16),
@@ -456,13 +454,13 @@
             dma(()),
             dma((n,)),
             dma(()),
-            dma((n, PARTS)),
+            dma((n, n)),
             dma(()),
             dma((n,)),
             dma(()),
             dma((n,)),
             dma(()),
-            dma((2, n2, PARTS)),
+            dma((2, n2, n)),
             dma(()),
             dma(()),
             dma(()),

time: 74.9 us -> 74.5 us (level)
  no operation moved by 1% of the time
where the time goes in v5:
time: 74.5 us; the launch traced here: 74.3 us
  Pallas kernels  73.7 us (99%)
    pallas_call x1, Pallas kernels, body(): pl.pallas_call(functools.partial(kernel, (nx, yl, n)), out_shape=(jax.Sha...  72.2 us
    pallas_call x1, Pallas kernels, body(): pl.pallas_call(settle, out_shape=tuple((jax.ShapeDtypeStruct(v.shape, v.d...  1.53 us

profile of v5, /device:TPU:1, one launch (start us, length us, event | category | flops | bytes accessed | tf_op | source)
XLA Modules:
  0.0 74.3 jit_solution(10271159417206955990)
XLA Ops:
  0.6 72.2 %shard_map.94 = (bf16[8,384]{1,0:T(8,128)(2,1)}, bf16[8,384]{1,0:T(8,128)(2,1)}, f32[2,8]{1,0:T(2,128)}) custom-call(s32[2,8]{1,0:T(2,128)} %bitcast.3, f32[2,8]{1,0:T(2,128)} %bitcast.4, bf16[8,384]{1,0:T(8,128)(2,1)} %tok_hbm.1, bf16[8,384]{1,0:T(8,128)(2,1)} %grad_hbm.1, bf16[6144,128]{1,0:T(8,128)(2,1)} %wg_hbm.1, bf16[6144,128]{1,0:T(8,128)(2,1)} %wu_hbm.1, ...), custom_call_target="tpu_custom_call" | custom-call | tf_op jit(solution)/shard_map/pallas_call | solution.py:418
  72.8 1.5 %shard_map.95 = (bf16[8,384]{1,0:T(8,128)(2,1)}, bf16[8,384]{1,0:T(8,128)(2,1)}, f32[2,8]{1,0:T(2,128)}) custom-call(bf16[8,384]{1,0:T(8,128)(2,1)} %get-tuple-element.9.mixed_in, bf16[8,384]{1,0:T(8,128)(2,1)} %get-tuple-element.10.tgrad_in, f32[2,8]{1,0:T(2,128)} %get-tuple-element.11.pgrad_in), custom_call_target="tpu_custom_call" | custom-call | tf_op jit(solution)/shard_map/pallas_call | solution.py:475
